TPU v7x, 32 devices: a whole 2x2x4 slice. The times are simulated.
32 devices in a mesh: row: 4 (over z), col: 8 (over y, x, core).
Axes of the slice: x: 2, y: 2, z: 4, core: 2. Of those that a mesh axis runs over, the one named last changes fastest.
Arguments:
- right_side: float32 [64, 16384], P(None, ('row', 'col')), may hold values from -80 to 80
- diag_vals: float32 [16384], P(('row', 'col')), may hold values from 1.05 to 1.6
- tiles: bfloat16 [64, 16, 256, 256], P(('row', 'col')), may hold values from -1 to 1, as said below
- col_ids: int32 [64, 16], P(('row', 'col')), may hold values from 0 to 63, as said below
Outputs:
- solution: float32 [64, 16384], P(None, ('row', 'col'))
- residual: float32 [64, 16384], P(None, ('row', 'col'))
Inputs may be any that keep to these rules, and one draw needn't show every extreme that they name: col_ids[i, m] = (i + o_m) mod 64 and col_ids[i, 8 + m] = (i - o_m) mod 64 for 8 distinct odd offsets o_m shared by all block-rows, each below 32. The pattern is symmetric. tiles[i, m] is the block in block-row i and block-column col_ids[i, m]; tiles[i, 8 + m] is the transpose of tiles[(i - o_m) mod 64, m], so the matrix is symmetric.
All inputs are finite; a program needn't handle non-finite values.
Results may differ from a plain program's by a relative error of at most 0.00062.
Values may be sent and summed in bfloat16 or wider, within the bound.
No kernel may reach another device: no remote copies, remote signals or barrier semaphores. Data moves between devices by JAX's collectives and lax.ppermute only.
A program may use at most 64 MiB of HBM per device.

v0:
```python
import jax
import jax.numpy as jnp
from jax import lax
from jax.sharding import PartitionSpec as P

ITERS = 4


def chol_solve(mat, rhs):
    lower = jnp.linalg.cholesky(mat)
    half = lax.linalg.triangular_solve(lower, rhs, left_side=True, lower=True)
    return lax.linalg.triangular_solve(lower, half, left_side=True, lower=True, transpose_a=True)


def gram_of(left, right):
    return jnp.dot(
        left, right.T, precision=lax.Precision.HIGHEST, preferred_element_type=jnp.float32
    )


def small_dot(left, right):
    return jnp.dot(left, right, precision=lax.Precision.HIGHEST, preferred_element_type=jnp.float32)


def apply_matrix(vec, diag_vals, tiles, col_ids):
    rhs_count = vec.shape[0]
    rows_here = tiles.shape[0]
    nbr = tiles.shape[1]
    blk = tiles.shape[2]
    rounded = vec.astype(jnp.bfloat16).reshape(rhs_count, rows_here, blk)
    whole = lax.all_gather(
        rounded.reshape(rhs_count, rows_here * blk), ("row", "col"), axis=1, tiled=True
    )
    whole = whole.reshape(rhs_count, -1, blk)
    picked = jnp.take(whole, col_ids.reshape(-1), axis=1).reshape(rhs_count, rows_here, nbr, blk)
    off = jnp.einsum("srkb,rkab->sra", picked, tiles, preferred_element_type=jnp.float32)
    coef = 1.0 / (nbr * blk)
    return diag_vals[None, :] * vec + coef * off.reshape(rhs_count, rows_here * blk)


def body(right_side, diag_vals, tiles, col_ids):
    solution = jnp.zeros_like(right_side)
    residual = right_side
    direction = right_side
    gram = lax.psum(gram_of(residual, residual), ("row", "col"))
    for step in range(ITERS):
        image = apply_matrix(direction, diag_vals, tiles, col_ids)
        curv = lax.psum(gram_of(direction, image), ("row", "col"))
        alpha = chol_solve(curv, gram)
        solution = solution + small_dot(alpha.T, direction)
        residual = residual - small_dot(alpha.T, image)
        if step + 1 < ITERS:
            gram_new = lax.psum(gram_of(residual, residual), ("row", "col"))
            beta = chol_solve(gram, gram_new)
            direction = residual + small_dot(beta.T, direction)
            gram = gram_new
    return (solution, residual)


def solution(mesh):
    placed = (
        P(None, ("row", "col")),
        P(("row", "col")),
        P(("row", "col"), None, None, None),
        P(("row", "col"), None),
    )
    return jax.shard_map(
        body,
        mesh=mesh,
        in_specs=placed,
        out_specs=(P(None, ("row", "col")), P(None, ("row", "col"))),
        check_vma=False,
    )
```

profile of v0, /device:TPU:0, one launch (start us, length us, event | category | flops | bytes accessed | tf_op | source)
XLA Modules:
  0.0 618.0 jit_solution(6379712227797717869)
XLA Ops:
  10.9 58.3 %all-gather.5.cloned.1.call-done = bf16[64,16384]{1,0:T(8,128)(2,1)} async-done(((bf16[64,512]{1,0:T(8,128)(2,1)}), bf16[64,16384]{1,0:T(8,128)(2,1)}) %all-gather.5.cloned.1.call-update) | async-done | bytes 2097168 | tf_op jit(solution)/shard_map/all_gather | solution.py:31
  75.8 40.2 %all-reduce = (f32[64,64]{0,1:T(8,128)S(1)}, f32[64,64]{0,1:T(8,128)S(1)}) all-reduce(f32[64,64]{0,1:T(8,128)S(1)} %fusion.64, f32[64,64]{0,1:T(8,128)S(1)} %convolution_bitcast_fusion.4), channel_id=1, replica_groups=mesh['row'=4,'col'=8] {'row','col'}, use_global_device_ids=true, to_apply=%region_3.6 | all-reduce | flops 8192 | bytes 65536 | tf_op jit(solution)/shard_map/psum | solution.py:45
  116.1 5.8 cholesky.119
  123.3 4.9 custom-call.21
  129.3 39.6 %psum.58 = f32[64,64]{0,1:T(8,128)S(1)} all-reduce(f32[64,64]{0,1:T(8,128)S(1)} %fusion.66), channel_id=1, replica_groups=mesh['row'=4,'col'=8] {'row','col'}, use_global_device_ids=true, to_apply=%region_4.9 | all-reduce | flops 4096 | bytes 32768 | tf_op jit(solution)/shard_map/psum | solution.py:53
  168.9 5.8 cholesky.130
  176.1 4.9 custom-call.23
  182.5 5.8 cholesky.152
  189.7 5.5 custom-call.27
  195.2 42.8 %all-gather.7.cloned.1.call-done = bf16[64,16384]{1,0:T(8,128)(2,1)} async-done(((bf16[64,512]{1,0:T(8,128)(2,1)}), bf16[64,16384]{1,0:T(8,128)(2,1)}) %all-gather.7.cloned.1.call-update) | async-done | bytes 2097168 | tf_op jit(solution)/shard_map/all_gather | solution.py:31
  244.6 40.0 %psum.59 = f32[64,64]{0,1:T(8,128)S(1)} all-reduce(f32[64,64]{0,1:T(8,128)S(1)} %fusion.8), channel_id=1, replica_groups=mesh['row'=4,'col'=8] {'row','col'}, use_global_device_ids=true, to_apply=%region_5.10 | all-reduce | flops 4096 | bytes 32768 | tf_op jit(solution)/shard_map/psum | solution.py:48
  284.7 5.8 cholesky.141
  291.9 4.9 custom-call.25
  297.8 39.6 %psum.60 = f32[64,64]{0,1:T(8,128)S(1)} all-reduce(f32[64,64]{0,1:T(8,128)S(1)} %fusion.67), channel_id=1, replica_groups=mesh['row'=4,'col'=8] {'row','col'}, use_global_device_ids=true, to_apply=%region_6.11 | all-reduce | flops 4096 | bytes 32768 | tf_op jit(solution)/shard_map/psum | solution.py:53
  339.0 5.8 cholesky.174
  346.1 5.5 custom-call.31
  351.6 42.8 %all-gather.9.cloned.1.call-done = bf16[64,16384]{1,0:T(8,128)(2,1)} async-done(((bf16[64,512]{1,0:T(8,128)(2,1)}), bf16[64,16384]{1,0:T(8,128)(2,1)}) %all-gather.9.cloned.1.call-update) | async-done | bytes 2097168 | tf_op jit(solution)/shard_map/all_gather | solution.py:31
  401.1 39.8 %psum.61 = f32[64,64]{0,1:T(8,128)S(1)} all-reduce(f32[64,64]{0,1:T(8,128)S(1)} %fusion.9), channel_id=1, replica_groups=mesh['row'=4,'col'=8] {'row','col'}, use_global_device_ids=true, to_apply=%region_7.12 | all-reduce | flops 4096 | bytes 32768 | tf_op jit(solution)/shard_map/psum | solution.py:48
  441.0 5.8 cholesky.163
  448.2 4.9 custom-call.29
  454.1 39.9 %psum.62 = f32[64,64]{1,0:T(8,128)S(1)} all-reduce(f32[64,64]{1,0:T(8,128)S(1)} %fusion.68), channel_id=1, replica_groups=mesh['row'=4,'col'=8] {'row','col'}, use_global_device_ids=true, to_apply=%region_8.13 | all-reduce | flops 4096 | bytes 32768 | tf_op jit(solution)/shard_map/psum | solution.py:53
  496.4 54.1 %all-gather.11.cloned.1.call-done = bf16[64,16384]{1,0:T(8,128)(2,1)} async-done(((bf16[64,512]{1,0:T(8,128)(2,1)}), bf16[64,16384]{1,0:T(8,128)(2,1)}) %all-gather.11.cloned.1.call-update) | async-done | bytes 2097168 | tf_op jit(solution)/shard_map/all_gather | solution.py:31
  557.1 39.8 %psum.63 = f32[64,64]{0,1:T(8,128)S(1)} all-reduce(f32[64,64]{0,1:T(8,128)S(1)} %fusion.10), channel_id=1, replica_groups=mesh['row'=4,'col'=8] {'row','col'}, use_global_device_ids=true, to_apply=%region_9.14 | all-reduce | flops 4096 | bytes 32768 | tf_op jit(solution)/shard_map/psum | solution.py:48
  597.0 5.8 cholesky.185
  (133 shorter events, 54.8 us)
Async XLA Ops:
  7.2 62.0 %all-gather.5.cloned.1.call-start = ((), (), s32[]{:S(2)}) async-start(), calls=%async_computation | async-start | bytes 2162688 | tf_op jit(solution)/shard_map/all_gather | solution.py:31
  8.8 229.2 %all-gather.7.cloned.1.call-start = ((), (), s32[]{:S(2)}) async-start(), calls=%async_computation.1 | async-start | bytes 2162688 | tf_op jit(solution)/shard_map/all_gather | solution.py:31
  71.7 3.8 copy-start
  71.7 3.8 copy-start.13
  128.6 109.4 %copy-start.9 = (f32[64,64]{1,0:T(8,128)}, f32[64,64]{1,0:T(8,128)S(1)}, u32[]{:S(2)}) copy-start(f32[64,64]{1,0:T(8,128)S(1)} %fusion.58) | copy-start | bytes 49156
  168.9 71.0 %copy-start.3 = (f32[64,64]{0,1:T(8,128)}, f32[64,64]{0,1:T(8,128)S(1)}, u32[]{:S(2)}) copy-start(f32[64,64]{0,1:T(8,128)S(1)} %psum.58) | copy-start | bytes 49156
  182.4 212.1 %all-gather.9.cloned.1.call-start = ((), (), s32[]{:S(2)}) async-start(), calls=%async_computation.2 | async-start | bytes 2162688 | tf_op jit(solution)/shard_map/all_gather | solution.py:31
  240.5 56.3 %copy-start.4 = (f32[64,64]{0,1:T(8,128)S(1)}, f32[64,64]{0,1:T(8,128)}, u32[]{:S(2)}) copy-start(f32[64,64]{0,1:T(8,128)} %copy-done.3) | copy-start | bytes 49156
  240.7 96.8 %copy-start.14 = (f32[1,64,64]{1,2,0:T(8,128)S(1)}, f32[1,64,64]{1,2,0:T(8,128)}, u32[]{:S(2)}) copy-start(f32[1,64,64]{1,2,0:T(8,128)} %custom-call.27) | copy-start | bytes 49156
  297.2 99.1 %copy-start.11 = (f32[64,64]{1,0:T(8,128)}, f32[64,64]{1,0:T(8,128)S(1)}, u32[]{:S(2)}) copy-start(f32[64,64]{1,0:T(8,128)S(1)} %fusion.48) | copy-start | bytes 49156
  297.5 98.8 %copy-start.1 = (f32[64,512]{1,0:T(8,128)}, f32[64,512]{1,0:T(8,128)S(1)}, u32[]{:S(2)}) copy-start(f32[64,512]{1,0:T(8,128)S(1)} %convolution_subtract_fusion.2) | copy-start | bytes 393220
  337.5 57.0 %copy-start.5 = (f32[64,64]{0,1:T(8,128)}, f32[64,64]{0,1:T(8,128)S(1)}, u32[]{:S(2)}) copy-start(f32[64,64]{0,1:T(8,128)S(1)} %psum.60) | copy-start | bytes 49156
  338.9 211.6 %all-gather.11.cloned.1.call-start = ((), (), s32[]{:S(2)}) async-start(), calls=%async_computation.3 | async-start | bytes 2162688 | tf_op jit(solution)/shard_map/all_gather | solution.py:31
  397.0 56.1 %copy-start.6 = (f32[64,64]{0,1:T(8,128)S(1)}, f32[64,64]{0,1:T(8,128)}, u32[]{:S(2)}) copy-start(f32[64,64]{0,1:T(8,128)} %copy-done.5) | copy-start | bytes 49156
  397.0 56.5 %copy-start.2 = (f32[64,512]{1,0:T(8,128)S(1)}, f32[64,512]{1,0:T(8,128)}, u32[]{:S(2)}) copy-start(f32[64,512]{1,0:T(8,128)} %copy-done.1) | copy-start | bytes 393220
  397.2 96.8 %copy-start.15 = (f32[1,64,64]{1,2,0:T(8,128)S(1)}, f32[1,64,64]{1,2,0:T(8,128)}, u32[]{:S(2)}) copy-start(f32[1,64,64]{1,2,0:T(8,128)} %custom-call.31) | copy-start | bytes 49156
  397.2 98.2 %copy-start.10 = (f32[64,64]{1,0:T(8,128)S(1)}, f32[64,64]{1,0:T(8,128)}, u32[]{:S(2)}) copy-start(f32[64,64]{1,0:T(8,128)} %copy-done.9) | copy-start | bytes 49156
  397.2 98.6 %copy-start.12 = (f32[64,64]{1,0:T(8,128)S(1)}, f32[64,64]{1,0:T(8,128)}, u32[]{:S(2)}) copy-start(f32[64,64]{1,0:T(8,128)} %copy-done.11) | copy-start | bytes 49156
  494.0 1.4 copy-start.7
  553.0 56.1 %copy-start.8 = (f32[64,64]{1,0:T(8,128)S(1)}, f32[64,64]{1,0:T(8,128)}, u32[]{:S(2)}) copy-start(f32[64,64]{1,0:T(8,128)} %copy-done.7) | copy-start | bytes 49156
Sparse Core Ops, SparseCore 0:
  11.5 57.6 all-gather.4
  182.5 55.4 all-gather.6
  339.0 55.4 all-gather.8
  495.5 54.9 all-gather.10
where the time goes:
time: 619 us; the launch traced here: 618 us
  blocking collectives  279 us (45%)
  waiting for transfers between devices  198 us (32%)
  other arithmetic  87.9 us (14%)
  matrix products  26.9 us (4%)
  between operations  14.6 us (2%)
  local copies, waits for them, and re-layouts  11.3 us (2%)
    all_gather x4, waiting for transfers between devices, apply_matrix(): lax.all_gather(rounded.reshape(rhs_count, rows_here * blk), ('row', 'col'...  198 us
    psum x3, blocking collectives, body(): curv = lax.psum(gram_of(direction, image), ('row', 'col'))  120 us
    psum x3, blocking collectives, body(): gram_new = lax.psum(gram_of(residual, residual), ('row', 'col'))  119 us
    another operation x21, other arithmetic, chol_solve(): lower = jnp.linalg.cholesky(mat)  45.6 us
    psum x1, blocking collectives, body(): gram = lax.psum(gram_of(residual, residual), ('row', 'col'))  40.2 us
    another operation x14, other arithmetic, chol_solve(): lax.linalg.triangular_solve(lower, half, left_side=True, lower=True, tran...  40 us
    dot_general x4, matrix products, apply_matrix(): jnp.einsum('srkb,rkab->sra', picked, tiles, preferred_element_type=jnp.fl...  14.3 us
  transfers between devices with their start and end apart: 4, of which 4 were waited for; matrix products, arithmetic and copies ran while one was open for 5% of the time, Pallas kernels for 0%

commit v1 on v0

--- a/solution.py
+++ b/solution.py
@@ -4,6 +4,12 @@
 from jax.sharding import PartitionSpec as P
 
 ITERS = 4
+
+
+def gather_and_add(value, name):
+    parts = lax.all_gather(value, name, axis=0, tiled=False)
+    total = parts.sum(axis=0)
+    return total
 
 
 def chol_solve(mat, rhs):
@@ -45,7 +51,7 @@
     gram = lax.psum(gram_of(residual, residual), ("row", "col"))
     for step in range(ITERS):
         image = apply_matrix(direction, diag_vals, tiles, col_ids)
-        curv = lax.psum(gram_of(direction, image), ("row", "col"))
+        curv = gather_and_add(gram_of(direction, image), ("row", "col"))
         alpha = chol_solve(curv, gram)
         solution = solution + small_dot(alpha.T, direction)
         residual = residual - small_dot(alpha.T, image)

time: 619 us -> 611 us (0.987)
  waiting for transfers between devices: 198 us -> 145 us
  blocking collectives: 279 us -> 324 us
    all_gather x0 -> x4, blocking collectives: none -> 170 us  [gather_and_add(): parts = lax.all_gather(value, name, axis=0, tiled=False)]
    psum x3 -> x0, blocking collectives: 120 us -> none  [body(): curv = lax.psum(gram_of(direction, image), ('row', 'col'))]
    all_gather x4, waiting for transfers between devices: 198 us -> 145 us  [apply_matrix(): lax.all_gather(rounded.reshape(rhs_count, rows_here * blk), ('row', 'col'...]
    psum x3, blocking collectives: 119 us -> 111 us  [body(): gram_new = lax.psum(gram_of(residual, residual), ('row', 'col'))]
  transfers between devices with their start and end apart: 4 -> 4, of which waited for: 4 -> 4; matrix products, arithmetic and copies ran while one was open for 5% -> 7% of each run, Pallas kernels for 0% -> 0%
where the time goes in v1:
time: 611 us; the launch traced here: 610 us
  blocking collectives  324 us (53%)
  waiting for transfers between devices  145 us (24%)
  other arithmetic  88.2 us (14%)
  matrix products  26.9 us (4%)
  between operations  14.5 us (2%)
  local copies, waits for them, and re-layouts  11.7 us (2%)
    all_gather x4, blocking collectives, gather_and_add(): parts = lax.all_gather(value, name, axis=0, tiled=False)  170 us
    all_gather x4, waiting for transfers between devices, apply_matrix(): lax.all_gather(rounded.reshape(rhs_count, rows_here * blk), ('row', 'col'...  145 us
    psum x3, blocking collectives, body(): gram_new = lax.psum(gram_of(residual, residual), ('row', 'col'))  111 us
    another operation x21, other arithmetic, chol_solve(): lower = jnp.linalg.cholesky(mat)  45.6 us
    psum x1, blocking collectives, body(): gram = lax.psum(gram_of(residual, residual), ('row', 'col'))  42.2 us
    another operation x14, other arithmetic, chol_solve(): lax.linalg.triangular_solve(lower, half, left_side=True, lower=True, tran...  40 us
    dot_general x4, matrix products, apply_matrix(): jnp.einsum('srkb,rkab->sra', picked, tiles, preferred_element_type=jnp.fl...  14.3 us
  transfers between devices with their start and end apart: 4, of which 4 were waited for; matrix products, arithmetic and copies ran while one was open for 7% of the time, Pallas kernels for 0%

profile of v1, /device:TPU:0, one launch (start us, length us, event | category | flops | bytes accessed | tf_op | source)
XLA Modules:
  0.0 610.3 jit_solution(7515138962895974362)
XLA Ops:
  10.8 42.2 %psum.28 = f32[64,64]{0,1:T(8,128)S(1)} all-reduce(f32[64,64]{0,1:T(8,128)S(1)} %fusion.64), channel_id=1, replica_groups=mesh['row'=4,'col'=8] {'row','col'}, use_global_device_ids=true, to_apply=%region_3.6 | all-reduce | flops 4096 | bytes 32768 | tf_op jit(solution)/shard_map/psum | solution.py:51
  53.1 5.8 cholesky.130
  60.3 4.9 custom-call.23
  75.9 42.6 %all-gather = f32[2048,64]{1,0:T(8,128)S(1)} all-gather(f32[64,64]{1,0:T(8,128)S(1)} %copy.76), channel_id=2, replica_groups=mesh['row'=4,'col'=8] {'row','col'}, dimensions={0}, use_global_device_ids=true | all-gather | bytes 540672 | tf_op jit(solution)/shard_map/all_gather | solution.py:10
  118.7 5.8 cholesky.119
  125.9 4.9 custom-call.21
  131.9 37.0 %psum.29 = f32[64,64]{0,1:T(8,128)S(1)} all-reduce(f32[64,64]{0,1:T(8,128)S(1)} %fusion.66), channel_id=1, replica_groups=mesh['row'=4,'col'=8] {'row','col'}, use_global_device_ids=true, to_apply=%region_4.9 | all-reduce | flops 4096 | bytes 32768 | tf_op jit(solution)/shard_map/psum | solution.py:59
  170.5 5.8 cholesky.152
  177.6 5.5 custom-call.27
  183.1 43.1 %all-gather.11.cloned.1.call-done = bf16[64,16384]{1,0:T(8,128)(2,1)} async-done(((bf16[64,512]{1,0:T(8,128)(2,1)}), bf16[64,16384]{1,0:T(8,128)(2,1)}) %all-gather.11.cloned.1.call-update) | async-done | bytes 2097168 | tf_op jit(solution)/shard_map/all_gather | solution.py:37
  232.7 42.7 %all-gather.1 = f32[2048,64]{1,0:T(8,128)S(1)} all-gather(f32[64,64]{1,0:T(8,128)S(1)} %fusion.8), channel_id=3, replica_groups=mesh['row'=4,'col'=8] {'row','col'}, dimensions={0}, use_global_device_ids=true | all-gather | bytes 540672 | tf_op jit(solution)/shard_map/all_gather | solution.py:10
  275.6 5.8 cholesky.141
  282.8 4.9 custom-call.25
  289.0 37.0 %psum.30 = f32[64,64]{0,1:T(8,128)S(1)} all-reduce(f32[64,64]{0,1:T(8,128)S(1)} %fusion.67), channel_id=1, replica_groups=mesh['row'=4,'col'=8] {'row','col'}, use_global_device_ids=true, to_apply=%region_6.11 | all-reduce | flops 4096 | bytes 32768 | tf_op jit(solution)/shard_map/psum | solution.py:59
  327.6 5.8 cholesky.174
  334.7 5.5 custom-call.31
  340.2 43.0 %all-gather.13.cloned.1.call-done = bf16[64,16384]{1,0:T(8,128)(2,1)} async-done(((bf16[64,512]{1,0:T(8,128)(2,1)}), bf16[64,16384]{1,0:T(8,128)(2,1)}) %all-gather.13.cloned.1.call-update) | async-done | bytes 2097168 | tf_op jit(solution)/shard_map/all_gather | solution.py:37
  389.9 42.5 %all-gather.2 = f32[2048,64]{1,0:T(8,128)S(1)} all-gather(f32[64,64]{1,0:T(8,128)S(1)} %fusion.9), channel_id=4, replica_groups=mesh['row'=4,'col'=8] {'row','col'}, dimensions={0}, use_global_device_ids=true | all-gather | bytes 540672 | tf_op jit(solution)/shard_map/all_gather | solution.py:10
  432.7 5.8 cholesky.163
  445.8 37.3 %psum.31 = f32[64,64]{1,0:T(8,128)S(1)} all-reduce(f32[64,64]{1,0:T(8,128)S(1)} %fusion.68), channel_id=1, replica_groups=mesh['row'=4,'col'=8] {'row','col'}, use_global_device_ids=true, to_apply=%region_8.13 | all-reduce | flops 4096 | bytes 32768 | tf_op jit(solution)/shard_map/psum | solution.py:59
  485.5 54.6 %all-gather.15.cloned.1.call-done = bf16[64,16384]{1,0:T(8,128)(2,1)} async-done(((bf16[64,512]{1,0:T(8,128)(2,1)}), bf16[64,16384]{1,0:T(8,128)(2,1)}) %all-gather.15.cloned.1.call-update) | async-done | bytes 2097168 | tf_op jit(solution)/shard_map/all_gather | solution.py:37
  546.6 42.5 %all-gather.3 = f32[2048,64]{1,0:T(8,128)S(1)} all-gather(f32[64,64]{1,0:T(8,128)S(1)} %fusion.10), channel_id=5, replica_groups=mesh['row'=4,'col'=8] {'row','col'}, dimensions={0}, use_global_device_ids=true | all-gather | bytes 540672 | tf_op jit(solution)/shard_map/all_gather | solution.py:10
  589.3 5.8 cholesky.185
  596.5 4.9 custom-call.33
  (140 shorter events, 59.6 us)
Async XLA Ops:
  7.2 62.1 %all-gather.9.cloned.1.call-start = ((), (), s32[]{:S(2)}) async-start(), calls=%async_computation | async-start | bytes 2162688 | tf_op jit(solution)/shard_map/all_gather | solution.py:37
  8.8 217.4 %all-gather.11.cloned.1.call-start = ((), (), s32[]{:S(2)}) async-start(), calls=%async_computation.1 | async-start | bytes 2162688 | tf_op jit(solution)/shard_map/all_gather | solution.py:37
  71.8 3.8 copy-start
  71.8 3.8 copy-start.13
  131.3 94.9 %copy-start.9 = (f32[64,64]{1,0:T(8,128)}, f32[64,64]{1,0:T(8,128)S(1)}, u32[]{:S(2)}) copy-start(f32[64,64]{1,0:T(8,128)S(1)} %fusion.58) | copy-start | bytes 49156
  168.9 59.1 %copy-start.3 = (f32[64,64]{0,1:T(8,128)}, f32[64,64]{0,1:T(8,128)S(1)}, u32[]{:S(2)}) copy-start(f32[64,64]{0,1:T(8,128)S(1)} %psum.29) | copy-start | bytes 49156
  170.3 213.0 %all-gather.13.cloned.1.call-start = ((), (), s32[]{:S(2)}) async-start(), calls=%async_computation.2 | async-start | bytes 2162688 | tf_op jit(solution)/shard_map/all_gather | solution.py:37
  228.9 58.9 %copy-start.4 = (f32[64,64]{0,1:T(8,128)S(1)}, f32[64,64]{0,1:T(8,128)}, u32[]{:S(2)}) copy-start(f32[64,64]{0,1:T(8,128)} %copy-done.3) | copy-start | bytes 49156
  228.9 97.2 %copy-start.14 = (f32[1,64,64]{1,2,0:T(8,128)S(1)}, f32[1,64,64]{1,2,0:T(8,128)}, u32[]{:S(2)}) copy-start(f32[1,64,64]{1,2,0:T(8,128)} %custom-call.27) | copy-start | bytes 49156
  288.2 0.6 copy-start.11
  288.8 94.5 %copy-start.1 = (f32[64,512]{1,0:T(8,128)}, f32[64,512]{1,0:T(8,128)S(1)}, u32[]{:S(2)}) copy-start(f32[64,512]{1,0:T(8,128)S(1)} %convolution_subtract_fusion.2) | copy-start | bytes 393220
  326.1 57.2 %copy-start.5 = (f32[64,64]{0,1:T(8,128)}, f32[64,64]{0,1:T(8,128)S(1)}, u32[]{:S(2)}) copy-start(f32[64,64]{0,1:T(8,128)S(1)} %psum.30) | copy-start | bytes 49156
  327.5 212.6 %all-gather.15.cloned.1.call-start = ((), (), s32[]{:S(2)}) async-start(), calls=%async_computation.3 | async-start | bytes 2162688 | tf_op jit(solution)/shard_map/all_gather | solution.py:37
  386.0 58.8 %copy-start.6 = (f32[64,64]{0,1:T(8,128)S(1)}, f32[64,64]{0,1:T(8,128)}, u32[]{:S(2)}) copy-start(f32[64,64]{0,1:T(8,128)} %copy-done.5) | copy-start | bytes 49156
  386.0 59.2 %copy-start.2 = (f32[64,512]{1,0:T(8,128)S(1)}, f32[64,512]{1,0:T(8,128)}, u32[]{:S(2)}) copy-start(f32[64,512]{1,0:T(8,128)} %copy-done.1) | copy-start | bytes 393220
  386.0 97.1 %copy-start.15 = (f32[1,64,64]{1,2,0:T(8,128)S(1)}, f32[1,64,64]{1,2,0:T(8,128)}, u32[]{:S(2)}) copy-start(f32[1,64,64]{1,2,0:T(8,128)} %custom-call.31) | copy-start | bytes 49156
  386.0 98.5 %copy-start.10 = (f32[64,64]{1,0:T(8,128)S(1)}, f32[64,64]{1,0:T(8,128)}, u32[]{:S(2)}) copy-start(f32[64,64]{1,0:T(8,128)} %copy-done.9) | copy-start | bytes 49156
  386.0 98.8 %copy-start.12 = (f32[64,64]{1,0:T(8,128)S(1)}, f32[64,64]{1,0:T(8,128)}, u32[]{:S(2)}) copy-start(f32[64,64]{1,0:T(8,128)} %copy-done.11) | copy-start | bytes 49156
  483.1 1.4 copy-start.7
  542.7 58.7 %copy-start.8 = (f32[64,64]{1,0:T(8,128)S(1)}, f32[64,64]{1,0:T(8,128)}, u32[]{:S(2)}) copy-start(f32[64,64]{1,0:T(8,128)} %copy-done.7) | copy-start | bytes 49156
Sparse Core Ops, SparseCore 0:
  11.5 57.7 all-gather.8
  170.4 55.7 all-gather.10
  327.6 55.6 all-gather.12
  484.6 55.4 all-gather.14
